TPU v7x, 256 devices: a whole 4x4x8 slice. The times are simulated.
256 devices in a mesh: lat: 64 (over x, y_lo, z), dp: 4 (over y_hi, core).
Axes of the slice: x: 4, y: 4 (y_hi: 2, y_lo: 2; y = y_hi * 2 + y_lo), z: 8, core: 2. Of those that a mesh axis runs over, the one named last changes fastest.
Arguments:
- inputs: bfloat16 [2048, 4096], P('dp', 'lat'), may hold values from -6 to 6
- dec_bias: bfloat16 [4096], P('lat'), may hold values from -3 to 3
- enc_weight: bfloat16 [4096, 16384], P(None, 'lat'), may hold values from -0.09375 to 0.09375
- enc_bias: float32 [16384], P('lat'), may hold values from -3 to 3
- dec_weight: bfloat16 [16384, 4096], P('lat'), may hold values from -0.046875 to 0.046875
- other_recon: float32 [2048, 4096], P('dp', 'lat'), may hold values from -6 to 6
- active_blocks: int32 [2048, 128], P('dp', 'lat'), may hold values 0 or 1
Outputs:
- error_full: float32 [2048, 4096], P('dp', 'lat')
- mse_loss: float32 [], replicated
- grad_dec: float32 [16384, 4096], P(('lat', 'dp'))
- grad_enc: float32 [4096, 16384], P(None, ('lat', 'dp'))
All inputs are finite; a program needn't handle non-finite values. No bound on the sum of `active_blocks` on one device may be relied on, other than what follows from the above.
Results may differ from a plain program's by a relative error of at most 0.0033.
Values may be sent and summed in bfloat16 or wider, within the bound.
A program may use at most 128 MiB of HBM per device.

v0:
```python
import jax
import jax.numpy as jnp
from jax import lax
from jax.sharding import PartitionSpec as P


def local(inputs, dec_bias, enc_weight, enc_bias, dec_weight, other_recon, active_blocks):
    row_count = inputs.shape[0]
    col_count = inputs.shape[1]
    block_size = enc_weight.shape[1] // active_blocks.shape[1]
    full_inputs, full_bias = (
        lax.all_gather(inputs, "lat", axis=1, tiled=True),
        lax.all_gather(dec_bias.reshape(1, -1), "lat", axis=1, tiled=True),
    )
    inputs_float = full_inputs.astype(jnp.float32)
    centered = (inputs_float - full_bias.astype(jnp.float32)).astype(jnp.bfloat16)
    pre_act = jnp.dot(centered, enc_weight, preferred_element_type=jnp.float32) + enc_bias[None, :]
    block_gate = (
        active_blocks.astype(jnp.float32)[:, :, None] * jnp.ones((1, 1, block_size), jnp.float32)
    ).reshape(row_count, -1)
    positive = jnp.maximum(pre_act, 0.0)
    activations = (positive * positive * block_gate).astype(jnp.bfloat16)
    outside = other_recon + dec_bias.astype(jnp.float32)[None, :]
    summed = lax.psum_scatter(
        lax.dot_general(
            dec_weight, activations, (((0,), (1,)), ((), ())), preferred_element_type=jnp.float32
        ),
        "lat",
        scatter_dimension=0,
        tiled=True,
    )
    error_local = summed.T + outside - inputs.astype(jnp.float32)
    error_bf = lax.all_gather(error_local.astype(jnp.bfloat16), "lat", axis=1, tiled=True)
    squares = lax.psum(jnp.sum(error_local * error_local), ("lat", "dp"))
    mse_loss = squares / (row_count * lax.axis_size("dp") * col_count * lax.axis_size("lat"))
    grad_dec = lax.psum_scatter(
        lax.dot_general(
            activations, error_bf, (((0,), (0,)), ((), ())), preferred_element_type=jnp.float32
        ),
        "dp",
        scatter_dimension=0,
        tiled=True,
    )
    dact = lax.dot_general(
        error_bf, dec_weight, (((1,), (1,)), ((), ())), preferred_element_type=jnp.float32
    )
    dpre = (dact * 2.0 * positive * block_gate).astype(jnp.bfloat16)
    enc_term = lax.dot_general(
        centered, dpre, (((0,), (0,)), ((), ())), preferred_element_type=jnp.float32
    )
    grad_enc = lax.psum_scatter(enc_term, "dp", scatter_dimension=1, tiled=True)
    return (error_local, mse_loss, grad_dec, grad_enc)


def solution(mesh):
    placed = (
        P("dp", "lat"),
        P("lat"),
        P(None, "lat"),
        P("lat"),
        P("lat", None),
        P("dp", "lat"),
        P("dp", "lat"),
    )
    return jax.shard_map(
        local,
        mesh=mesh,
        in_specs=placed,
        out_specs=(P("dp", "lat"), P(), P(("lat", "dp"), None), P(None, ("lat", "dp"))),
        check_vma=False,
    )
```

profile of v0, /device:TPU:1, one launch (start us, length us, event | category | flops | bytes accessed | tf_op | source)
XLA Modules:
  0.0 1096.9 jit_solution(8180831337322198771)
XLA Ops:
  7.2 0.0 all-gather.4.cloned.1.call-start
  7.2 0.7 all-gather.4.cloned.1.call-update
  7.9 0.0 reduce-scatter.10.cloned.1.call-start
  8.0 0.7 convert_element_type.27
  8.7 0.1 copy.15
  8.8 1.3 dynamic-slice
  10.8 0.9 dynamic-update-slice
  11.6 139.7 %all-reduce = bf16[4096]{0:T(1024)(128)(2,1)S(1)} all-reduce(bf16[4096]{0:T(1024)(128)(2,1)S(1)} %dynamic-update-slice), channel_id=2, replica_groups=mesh['lat'=64,'dp'=4] {'lat'}, use_global_device_ids=true, to_apply=%add | all-reduce | flops 4096 | bytes 16384
  151.4 123.1 %all-gather.4.cloned.1.call-done = bf16[512,4096]{0,1:T(8,128)(2,1)} async-done(((bf16[512,64]{0,1:T(8,128)(2,1)}), bf16[512,4096]{0,1:T(8,128)(2,1)}) %all-gather.4.cloned.1.call-update) | async-done | bytes 4194320 | tf_op jit(solution)/shard_map/all_gather | solution.py:12
  274.5 0.6 mul.27
  275.1 5.8 fusion.8
  280.8 4.5 convolution_bitcast_fusion
  285.3 9.0 copy.20
  294.3 0.0 reduce-scatter.10.cloned.1.call-update
  294.4 0.0 all-gather.6.cloned.1.call-start
  294.4 0.8 copy-done.2
  295.2 0.1 copy.17
  295.3 0.1 copy.16
  295.5 324.6 %reduce-scatter.10.cloned.1.call-done = f32[64,512]{1,0:T(8,128)} async-done(((f32[4096,512]{1,0:T(8,128)}), f32[64,512]{1,0:T(8,128)}) %reduce-scatter.10.cloned.1.call-update) | async-done | bytes 131088
  620.1 1.0 copy.21
  621.2 0.7 copy.18
  621.9 0.0 all-gather.6.cloned.1.call-update
  621.9 0.0 reduce-scatter.8.cloned.1.call-start
  622.0 300.7 %all-gather.6.cloned.1.call-done = bf16[512,4096]{0,1:T(8,128)(2,1)} async-done(((bf16[512,64]{0,1:T(8,128)(2,1)}), bf16[512,4096]{0,1:T(8,128)(2,1)}) %all-gather.6.cloned.1.call-update) | async-done | bytes 4194320 | tf_op jit(solution)/shard_map/all_gather | solution.py:33
  922.7 10.2 fusion
  932.9 0.0 reduce-scatter.6.cloned.1.call-start
  933.0 5.4 fusion.15
  938.5 0.7 multiply_reduce_fusion
  939.1 117.6 %psum.7 = f32[]{:T(128)} all-reduce(f32[]{:T(128)} %multiply_reduce_fusion), channel_id=1, replica_groups=mesh['lat'=64,'dp'=4] {'lat','dp'}, use_global_device_ids=true, to_apply=%region_2.0 | all-reduce | flops 1 | bytes 8 | tf_op jit(solution)/shard_map/psum | solution.py:34
  1056.8 0.8 copy.19
  1058.2 0.0 reduce-scatter.8.cloned.1.call-done
  1058.2 31.0 %reduce-scatter.6.cloned.1.call-done = f32[64,4096]{1,0:T(8,128)} async-done(((f32[256,4096]{1,0:T(8,128)}), f32[64,4096]{1,0:T(8,128)}) %reduce-scatter.6.cloned.1.call-update) | async-done | bytes 1048592 | tf_op jit(solution)/shard_map/reduce_scatter | solution.py:36
  (15 shorter events, 0.1 us)
Async XLA Ops:
  7.2 273.7 %copy-start = (bf16[256,4096]{1,0:T(8,128)(2,1)S(1)}, bf16[256,4096]{1,0:T(8,128)(2,1)}, u32[]{:S(2)}) copy-start(bf16[256,4096]{1,0:T(8,128)(2,1)} %param.11) | copy-start | bytes 6291460
  7.2 267.3 %all-gather.4.cloned.1.call-start = ((), (), s32[]{:S(2)}) async-start(), calls=%async_computation.3 | async-start | bytes 4259840 | tf_op jit(solution)/shard_map/all_gather | solution.py:12
  7.9 612.2 %reduce-scatter.10.cloned.1.call-start = ((), (), s32[]{:S(2)}) async-start(), calls=%async_computation.7 | async-start | bytes 8519680
  275.1 5.8 copy-start.1
  294.3 0.8 copy-start.2
  294.3 1.0 copy-start.4
  294.3 1.0 copy-start.3
  294.4 628.3 %all-gather.6.cloned.1.call-start = ((), (), s32[]{:S(2)}) async-start(), calls=%async_computation.4 | async-start | bytes 4259840 | tf_op jit(solution)/shard_map/all_gather | solution.py:33
  621.9 436.3 %reduce-scatter.8.cloned.1.call-start = ((), (), s32[]{:S(2)}) async-start(), calls=%async_computation.6 | async-start | bytes 5242880 | tf_op jit(solution)/shard_map/reduce_scatter | solution.py:51
  932.9 156.3 %reduce-scatter.6.cloned.1.call-start = ((), (), s32[]{:S(2)}) async-start(), calls=%async_computation.5 | async-start | bytes 5242880 | tf_op jit(solution)/shard_map/reduce_scatter | solution.py:36
Sparse Core Ops, SparseCore 0:
  9.8 264.6 all-gather.3
  294.5 325.5 reduce-scatter.9
  622.4 300.1 all-gather.5
  933.1 96.8 reduce-scatter.7
  1033.4 55.7 reduce-scatter.5
where the time goes:
time: 1100 us
  waiting for transfers between devices  780 us (71%)
  blocking collectives  257 us (23%)
  matrix products  25.9 us (2%)
  between operations  16.3 us (1%)
  local copies, waits for them, and re-layouts  15.4 us (1%)
    unnamed x6, waiting for transfers between devices  325 us
    all_gather x1, waiting for transfers between devices, local(): lax.all_gather(error_local.astype(jnp.bfloat16), 'lat', axis=1, tiled=True)  301 us
    unnamed x1, blocking collectives  140 us
    all_gather x1, waiting for transfers between devices, local(): lax.all_gather(inputs, 'lat', axis=1, tiled=True)  123 us
    psum x1, blocking collectives, local(): squares = lax.psum(jnp.sum(error_local * error_local), ('lat', 'dp'))  118 us
    reduce_scatter x1, waiting for transfers between devices, local(): lax.psum_scatter(lax.dot_general(activations, error_bf, (((0,), (0,)), ((...  31 us
  transfers between devices with their start and end apart: 5, of which 4 were waited for; matrix products, arithmetic and copies ran while one was open for 1% of the time, Pallas kernels for 0%

commit v1 on v0

--- a/solution.py
+++ b/solution.py
@@ -30,7 +30,12 @@
         tiled=True,
     )
     error_local = summed.T + outside - inputs.astype(jnp.float32)
-    error_bf = lax.all_gather(error_local.astype(jnp.bfloat16), "lat", axis=1, tiled=True)
+    error_bf = jnp.concatenate(
+        lax.all_to_all(
+            jnp.stack([error_local.astype(jnp.bfloat16)] * lax.axis_size("lat")), "lat", 0, 0
+        ),
+        axis=1,
+    )
     squares = lax.psum(jnp.sum(error_local * error_local), ("lat", "dp"))
     mse_loss = squares / (row_count * lax.axis_size("dp") * col_count * lax.axis_size("lat"))
     grad_dec = lax.psum_scatter(

time: 1100 us -> 868 us (0.79)
  waiting for transfers between devices: 780 us -> 479 us
  blocking collectives: 257 us -> 330 us
    all_gather x1 -> x0, waiting for transfers between devices: 301 us -> none  [local(): lax.all_gather(error_local.astype(jnp.bfloat16), 'lat', axis=1, tiled=True)]
    all_to_all x0 -> x1, blocking collectives: none -> 57.4 us  [local(): lax.all_to_all(jnp.stack([error_local.astype(jnp.bfloat16)] * lax.axis_si...]
    psum x1, blocking collectives: 118 us -> 133 us  [local(): squares = lax.psum(jnp.sum(error_local * error_local), ('lat', 'dp'))]
    unnamed x6 -> x5, waiting for transfers between devices: 325 us -> 325 us
  transfers between devices with their start and end apart: 5 -> 4, of which waited for: 4 -> 3; matrix products, arithmetic and copies ran while one was open for 1% -> 1% of each run, Pallas kernels for 0% -> 0%
where the time goes in v1:
time: 868 us
  waiting for transfers between devices  479 us (55%)
  blocking collectives  330 us (38%)
  matrix products  25.8 us (3%)
  between operations  16.3 us (2%)
  local copies, waits for them, and re-layouts  15.3 us (2%)
    unnamed x5, waiting for transfers between devices  325 us
    unnamed x1, blocking collectives  140 us
    psum x1, blocking collectives, local(): squares = lax.psum(jnp.sum(error_local * error_local), ('lat', 'dp'))  133 us
    all_gather x1, waiting for transfers between devices, local(): lax.all_gather(inputs, 'lat', axis=1, tiled=True)  123 us
    all_to_all x1, blocking collectives, local(): lax.all_to_all(jnp.stack([error_local.astype(jnp.bfloat16)] * lax.axis_si...  57.4 us
    reduce_scatter x1, waiting for transfers between devices, local(): lax.psum_scatter(lax.dot_general(activations, error_bf, (((0,), (0,)), ((...  30.5 us
  transfers between devices with their start and end apart: 4, of which 3 were waited for; matrix products, arithmetic and copies ran while one was open for 1% of the time, Pallas kernels for 0%

profile of v1, /device:TPU:1, one launch (start us, length us, event | category | flops | bytes accessed | tf_op | source)
XLA Modules:
  0.0 867.7 jit_solution(4835640428335427953)
XLA Ops:
  7.2 0.0 all-gather.3.cloned.1.call-start
  7.2 0.7 all-gather.3.cloned.1.call-update
  7.9 0.0 reduce-scatter.10.cloned.1.call-start
  8.0 0.7 convert_element_type.27
  8.7 0.1 copy.20
  8.8 1.3 dynamic-slice
  10.8 0.9 dynamic-update-slice
  11.6 139.7 %all-reduce = bf16[4096]{0:T(1024)(128)(2,1)S(1)} all-reduce(bf16[4096]{0:T(1024)(128)(2,1)S(1)} %dynamic-update-slice), channel_id=2, replica_groups=mesh['lat'=64,'dp'=4] {'lat'}, use_global_device_ids=true, to_apply=%add | all-reduce | flops 4096 | bytes 16384
  151.4 123.1 %all-gather.3.cloned.1.call-done = bf16[512,4096]{0,1:T(8,128)(2,1)} async-done(((bf16[512,64]{0,1:T(8,128)(2,1)}), bf16[512,4096]{0,1:T(8,128)(2,1)}) %all-gather.3.cloned.1.call-update) | async-done | bytes 4194320 | tf_op jit(solution)/shard_map/all_gather | solution.py:12
  274.5 0.6 mul.27
  275.1 5.8 fusion.8
  280.8 4.5 convolution_bitcast_fusion
  285.3 9.0 %copy.25 = f32[4096,512]{1,0:T(8,128)} copy(f32[4096,512]{0,1:T(8,128)} %convolution_bitcast_fusion) | data formatting | bytes 16777216
  294.4 0.0 reduce-scatter.10.cloned.1.call-update
  294.4 0.0 reduce-scatter.8.cloned.1.call-start
  294.4 0.8 copy-done.3
  295.2 0.1 copy.22
  295.4 0.1 copy.21
  295.5 324.6 %reduce-scatter.10.cloned.1.call-done = f32[64,512]{1,0:T(8,128)} async-done(((f32[4096,512]{1,0:T(8,128)}), f32[64,512]{1,0:T(8,128)}) %reduce-scatter.10.cloned.1.call-update) | async-done | bytes 131088
  620.1 1.0 copy.26
  621.1 0.1 fusion.13
  621.2 0.1 copy.23
  621.3 0.5 stack.2
  621.8 57.4 %all_to_all.5 = bf16[64,512,64]{1,2,0:T(8,128)(2,1)} all-to-all(bf16[64,512,64]{1,2,0:T(8,128)(2,1)S(1)} %stack.2), channel_id=1, replica_groups=mesh['lat'=64,'dp'=4] {'lat'}, dimensions={0} | all-to-all | bytes 8388608 | tf_op jit(solution)/shard_map/all_to_all | solution.py:34
  679.2 10.1 %fusion = f32[4096,256]{0,1:T(8,128)} fusion(bf16[512,4096]{0,1:T(8,128)(2,1)} %all-gather.3.cloned.1.call-done, f32[4096]{0:T(1024)S(1)} %sub.22, f32[512,256]{1,0:T(8,128)} %get-tuple-element.19, bf16[512,4096]{0,1:T(8,128)(2,1)} %bitcast.28, bf16[256,4096]{1,0:T(8,128)(2,1)S(1)} %copy-done, f32[64,8,2,128]{3,2,1,0:T(2,128)S(1)} %bitcast.31), kind=kOutput, calls=%fused_computation.2 | convolution fusion | flops 2154299392 | bytes 15745024 | tf_op jit(solution)/shard_map/dot_general | solution.py:53
  689.3 0.0 reduce-scatter.6.cloned.1.call-start
  689.4 5.5 fusion.15
  694.8 0.7 multiply_reduce_fusion
  695.5 132.7 %psum.7 = f32[]{:T(128)} all-reduce(f32[]{:T(128)} %multiply_reduce_fusion), channel_id=1, replica_groups=mesh['lat'=64,'dp'=4] {'lat','dp'}, use_global_device_ids=true, to_apply=%region_2.0 | all-reduce | flops 1 | bytes 8 | tf_op jit(solution)/shard_map/psum | solution.py:39
  828.2 0.8 copy.24
  829.6 0.0 reduce-scatter.8.cloned.1.call-done
  829.6 30.5 %reduce-scatter.6.cloned.1.call-done = f32[64,4096]{1,0:T(8,128)} async-done(((f32[256,4096]{1,0:T(8,128)}), f32[64,4096]{1,0:T(8,128)}) %reduce-scatter.6.cloned.1.call-update) | async-done | bytes 1048592 | tf_op jit(solution)/shard_map/reduce_scatter | solution.py:41
  (16 shorter events, 0.1 us)
Async XLA Ops:
  7.2 273.7 %copy-start = (bf16[256,4096]{1,0:T(8,128)(2,1)S(1)}, bf16[256,4096]{1,0:T(8,128)(2,1)}, u32[]{:S(2)}) copy-start(bf16[256,4096]{1,0:T(8,128)(2,1)} %param.11) | copy-start | bytes 6291460
  7.2 267.3 %all-gather.3.cloned.1.call-start = ((), (), s32[]{:S(2)}) async-start(), calls=%async_computation.4 | async-start | bytes 4259840 | tf_op jit(solution)/shard_map/all_gather | solution.py:12
  7.9 612.2 %reduce-scatter.10.cloned.1.call-start = ((), (), s32[]{:S(2)}) async-start(), calls=%async_computation.7 | async-start | bytes 8519680
  275.1 5.8 copy-start.1
  294.4 0.8 copy-start.3
  294.4 1.0 copy-start.5
  294.4 1.0 copy-start.4
  294.4 535.2 %reduce-scatter.8.cloned.1.call-start = ((), (), s32[]{:S(2)}) async-start(), calls=%async_computation.6 | async-start | bytes 5242880 | tf_op jit(solution)/shard_map/reduce_scatter | solution.py:56
  621.8 57.4 %copy-start.2 = (f32[512,2,128]{2,1,0:T(2,128)S(1)}, f32[512,2,128]{2,1,0:T(2,128)}, u32[]{:S(2)}) copy-start(f32[512,2,128]{2,1,0:T(2,128)} %copy-done.1) | copy-start | bytes 1572868
  689.3 170.8 %reduce-scatter.6.cloned.1.call-start = ((), (), s32[]{:S(2)}) async-start(), calls=%async_computation.5 | async-start | bytes 5242880 | tf_op jit(solution)/shard_map/reduce_scatter | solution.py:41
Sparse Core Ops, SparseCore 0:
  9.8 264.6 all-gather.2
  294.5 325.5 reduce-scatter.9
  689.4 111.2 reduce-scatter.7
  804.1 55.9 reduce-scatter.5
